TPU v7x, 128 devices: a whole 4x4x4 slice. The times are simulated.
128 devices in a mesh: row: 8 (over z, core), col: 16 (over y, x).
Axes of the slice: x: 4, y: 4, z: 4, core: 2. Of those that a mesh axis runs over, the one named last changes fastest.
Arguments:
- hidden: bfloat16 [1408, 16384], P('col', 'row'), may hold values from -18 to 18
- gain_in: bfloat16 [1408], replicated, may hold values from 0.5 to 1.5
- w_query: bfloat16 [1408, 1408], P('col'), may hold values from -0.3125 to 0.3125
- w_pair: bfloat16 [2, 1408, 1408], P(None, 'col'), may hold values from -0.15625 to 0.15625
- kv_cache: bfloat16 [2, 1408, 16384], P(None, 'col', 'row'), may hold values from -103 to 103
- recompute_rows: int32 [8, 200], P('row'), may hold values from 0 to 2047, as said below
- segment_ids: int32 [16384], P('row'), may hold values from -1 to 1, as said below
- w_out: bfloat16 [1408, 1408], P('col'), may hold values from -0.3125 to 0.3125
- gain_merge: bfloat16 [1408], replicated, may hold values from 0.5 to 1.5
- w_merge: bfloat16 [4, 1408, 1408], P(None, 'col'), may hold values from -0.078125 to 0.078125
- requests: int32 [8, 16, 85], P('row'), may hold values from -1 to 511, as said below
Outputs:
- delivered: bfloat16 [8, 16, 85, 1408], P('row', 'col')
Inputs may be any that keep to these rules, and one draw needn't show every extreme that they name: `segment_ids`: ids do not fall along the tokens except to -1 for the padding at the end; every image covers a multiple of 4 tokens and starts at a multiple of 4. `recompute_rows`: the 200 offsets of one index of row are distinct. `requests`: for each index of row, the lists of all owners together name each of its 512 merged tokens exactly once; unused slots hold -1 and follow the used ones.
All inputs are finite; a program needn't handle non-finite values.
Results may differ from a plain program's by a relative error of at most 0.025.
The roundings to bfloat16 on the way count: a program that leaves them out, or rounds other values in their place, can miss the bound.
Values may be sent and summed in bfloat16 or wider, within the bound.
A program may use at most 128 MiB of HBM per device.

v0:
```python
import jax
import jax.numpy as jnp
from jax import lax
from jax.sharding import PartitionSpec as P

HD = 88
EPSILON = 1e-06
MASKED = -1e30
KEY_BLOCK = 1024


def on_device(
    hidden,
    gain_in,
    w_query,
    w_pair,
    kv_cache,
    recompute_rows,
    segment_ids,
    w_out,
    gain_merge,
    w_merge,
    requests,
):
    local_width, tok_rows = hidden.shape
    model_width = w_query.shape[1]
    n_col = model_width // local_width
    heads_here = local_width // HD
    score_scale = HD ** (-0.5)
    col_index = lax.axis_index("col")
    full_rows = lax.all_gather(hidden, "col", axis=0, tiled=True)
    out_weight = lax.all_gather(w_out, "col", axis=0, tiled=True)
    full_float = full_rows.astype(jnp.float32)
    in_mean = jnp.sum(full_float, axis=0, keepdims=True) / model_width
    in_square = jnp.sum(full_float * full_float, axis=0, keepdims=True) / model_width
    normed = (
        (full_float - in_mean)
        * lax.rsqrt(in_square - in_mean * in_mean + EPSILON)
        * gain_in.astype(jnp.float32)[:, None]
    ).astype(jnp.bfloat16)
    queries = jnp.dot(w_query, normed, preferred_element_type=jnp.float32).astype(jnp.bfloat16)
    picked_rows = recompute_rows[0]
    normed_picked = jnp.take(normed, picked_rows, axis=1)
    fresh_pairs = jnp.dot(
        w_pair.reshape(2 * local_width, model_width),
        normed_picked,
        preferred_element_type=jnp.float32,
    )
    fresh_pairs = fresh_pairs.astype(jnp.bfloat16).reshape(2, local_width, -1)
    keys_values = kv_cache.at[:, :, picked_rows].set(fresh_pairs)
    query_heads = queries.reshape(heads_here, HD, tok_rows)
    pair_local = jnp.concatenate(
        [keys_values.reshape(2 * local_width, tok_rows), segment_ids.astype(jnp.bfloat16)[None, :]],
        axis=0,
    )
    pair_all = lax.all_gather(pair_local, "row", axis=1, tiled=True)
    pair_rows = pair_all[: 2 * local_width].reshape(2, local_width, -1)
    segment_line = pair_all[2 * local_width].astype(jnp.int32)

    def take_block(carried, pair_block, segment_block):
        running_max, running_sum, weighted = carried
        key_block = pair_block[0].reshape(heads_here, HD, -1)
        value_block = pair_block[1].reshape(heads_here, HD, -1)
        scores = (
            jnp.einsum("hdq,hdk->hqk", query_heads, key_block, preferred_element_type=jnp.float32)
            * score_scale
        )
        allowed = (segment_ids[:, None] == segment_block[None, :])[None, :, :]
        new_max = jnp.maximum(running_max, jnp.max(jnp.where(allowed, scores, MASKED), axis=2))
        weights_exp = jnp.where(allowed, jnp.exp(scores - new_max[:, :, None]), 0.0)
        factor = jnp.exp(running_max - new_max)
        running_sum = running_sum * factor + jnp.sum(weights_exp, axis=2)
        product = jnp.einsum(
            "hqk,hdk->hdq",
            weights_exp.astype(jnp.bfloat16),
            value_block,
            preferred_element_type=jnp.float32,
        )
        weighted = weighted * factor[:, None, :] + product
        return (new_max, running_sum, weighted)

    starting = (
        jnp.full((heads_here, tok_rows), MASKED, jnp.float32),
        jnp.zeros((heads_here, tok_rows), jnp.float32),
        jnp.zeros((heads_here, HD, tok_rows), jnp.float32),
    )
    piece_rows = pair_rows.shape[2]
    whole_blocks = piece_rows // KEY_BLOCK

    def loop_body(block_index, loop_state):
        pair_block = lax.dynamic_slice_in_dim(pair_rows, block_index * KEY_BLOCK, KEY_BLOCK, 2)
        segment_block = lax.dynamic_slice_in_dim(
            segment_line, block_index * KEY_BLOCK, KEY_BLOCK, 0
        )
        return take_block(loop_state, pair_block, segment_block)

    running_max, running_sum, weighted = lax.fori_loop(0, whole_blocks, loop_body, starting)
    attended = (
        (weighted / running_sum[:, None, :]).astype(jnp.bfloat16).reshape(local_width, tok_rows)
    )
    chunk = tok_rows // n_col
    attended_chunk = lax.all_to_all(attended, "col", 1, 0, tiled=True)
    x_chunk = lax.dynamic_slice_in_dim(full_float, col_index * chunk, chunk, 1)
    projected = lax.dot_general(
        out_weight, attended_chunk, (((0,), (0,)), ((), ())), preferred_element_type=jnp.float32
    )
    updated = x_chunk + projected
    row_mean = jnp.sum(updated, axis=0, keepdims=True) / model_width
    row_square = jnp.sum(updated * updated, axis=0, keepdims=True) / model_width
    merger_chunk = (
        (updated - row_mean)
        * lax.rsqrt(row_square - row_mean * row_mean + EPSILON)
        * gain_merge.astype(jnp.float32)[:, None]
    ).astype(jnp.bfloat16)
    merge_weight, _ = lax.optimization_barrier((w_merge, pair_all))
    merge_full = lax.all_gather(merge_weight, "col", axis=1, tiled=True)
    grouped = merger_chunk.reshape(model_width, chunk // 4, 4)
    merged_here = jnp.einsum("fgi,ifd->gd", grouped, merge_full, preferred_element_type=jnp.float32)
    merged_all = lax.all_gather(merged_here.astype(jnp.bfloat16), "col", axis=0, tiled=True)
    wanted_rows = lax.dynamic_index_in_dim(requests[0], col_index, 0, keepdims=False)
    is_valid = wanted_rows >= 0
    safe_index = jnp.where(is_valid, wanted_rows, 0)
    picked = jnp.where(is_valid[:, None], merged_all[safe_index], jnp.zeros((), jnp.bfloat16))
    return picked.reshape(1, 1, picked.shape[0], model_width)


def solution(mesh):
    placed = (
        P("col", "row"),
        P(),
        P("col", None),
        P(None, "col", None),
        P(None, "col", "row"),
        P("row", None),
        P("row"),
        P("col", None),
        P(),
        P(None, "col", None),
        P("row", None, None),
    )
    return jax.shard_map(
        on_device,
        mesh=mesh,
        in_specs=placed,
        out_specs=P("row", "col", None, None),
        check_vma=False,
    )
```

profile of v0, /device:TPU:0, one launch (start us, length us, event | category | flops | bytes accessed | tf_op | source)
XLA Modules:
  0.0 484.3 jit_solution(13265763063287293929)
XLA Ops:
  12.5 58.2 %all-gather.6.cloned.1.call-done = bf16[1408,2048]{1,0:T(8,128)(2,1)} async-done(((bf16[88,2048]{1,0:T(8,128)(2,1)}), bf16[1408,2048]{1,0:T(8,128)(2,1)}) %all-gather.6.cloned.1.call-update) | async-done | bytes 5767184 | tf_op jit(solution)/shard_map/all_gather | solution.py:31
  70.7 8.3 %copy.28 = bf16[1408,2048]{0,1:T(8,128)(2,1)} copy(bf16[1408,2048]{1,0:T(8,128)(2,1)} %all-gather.6.cloned.1.call-done) | data formatting | bytes 11534336 | tf_op jit(solution)/shard_map/all_gather | solution.py:31
  93.2 6.9 %scatter_fusion = bf16[2,88,2048]{1,0,2:T(2,128)(2,1)S(1)} fusion(bf16[2,88,2048]{1,0,2:T(2,128)(2,1)S(1)} %copy.30, s32[200]{0:T(256)S(1)} %bitcast.122, bf16[200,2,88]{2,1,0:T(2,128)(2,1)S(1)} %bitcast.115), kind=kCustom, calls=%fused_computation.2 | custom fusion | bytes 212000 | tf_op jit(solution)/shard_map/scatter | solution.py:50
  107.5 34.2 %all-gather.8.cloned.1.call-done = bf16[177,16384]{1,0:T(8,128)(2,1)} async-done(((bf16[177,2048]{1,0:T(8,128)(2,1)}), bf16[177,16384]{1,0:T(8,128)(2,1)}) %all-gather.8.cloned.1.call-update) | async-done | bytes 5799952 | tf_op jit(solution)/shard_map/all_gather | solution.py:56
  141.7 5.8 %slice.29 = bf16[176,16384]{1,0:T(8,128)(2,1)} slice(bf16[177,16384]{1,0:T(8,128)(2,1)} %all-gather.8.cloned.1.call-done), slice={[0:176], [0:16384]} | slice | bytes 11534336 | tf_op jit(solution)/shard_map/slice | solution.py:57
  148.5 254.0 %while.18 = (s32[]{:T(128)}, f32[1,2048]{1,0:T(1,128)S(1)}, f32[1,2048]{1,0:T(1,128)S(1)}, f32[1,88,2048]{2,1,0:T(8,128)S(1)}, s32[2048]{0:T(1024)S(1)}, /*index...) while((s32[]{:T(128)}, f32[1,2048]{1,0:T(1,128)S(1)}, ...), condition=%wide.region_6.7_spmd.clone, body=%wide.region_3.0_spmd.clone.sunk | while | flops 768108544 | bytes 27504848 | solution.py:97
  164.3 5.6 %fusion.45 = (f32[2048]{0:T(1024)S(1)}, f32[1024,2048]{1,0:T(8,128)}) fusion(s32[2048]{0:T(1024)S(1)} %get-tuple-element.292, s32[1024]{0:T(1024)S(1)} %dynamic_slice.32, bf16[1,88,2048]{2,1,0:T(8,128)(2,1)S(1)} %get-tuple-element.295, bf16[2,88,16384]{2,1,0:T(8,128)(2,1)} %get-tuple-element.294, s32[]{:T(128)S(6)} %select_n.132), kind=kOutput, calls=%fused_computation.5.clone.1 | convolution fusion | flops 377485312 | bytes 8949764 | tf_op jit(solution)/shard_map/while/body/eval_jaxpr/hdq,hdk->hqk/dot_general | solution.py:65
  180.0 5.6 %fusion.45 = (f32[2048]{0:T(1024)S(1)}, f32[1024,2048]{1,0:T(8,128)}) fusion(s32[2048]{0:T(1024)S(1)} %get-tuple-element.292, s32[1024]{0:T(1024)S(1)} %dynamic_slice.32, bf16[1,88,2048]{2,1,0:T(8,128)(2,1)S(1)} %get-tuple-element.295, bf16[2,88,16384]{2,1,0:T(8,128)(2,1)} %get-tuple-element.294, s32[]{:T(128)S(6)} %select_n.132), kind=kOutput, calls=%fused_computation.5.clone.1 | convolution fusion | flops 377485312 | bytes 8949764 | tf_op jit(solution)/shard_map/while/body/eval_jaxpr/hdq,hdk->hqk/dot_general | solution.py:65
  195.8 5.6 %fusion.45 = (f32[2048]{0:T(1024)S(1)}, f32[1024,2048]{1,0:T(8,128)}) fusion(s32[2048]{0:T(1024)S(1)} %get-tuple-element.292, s32[1024]{0:T(1024)S(1)} %dynamic_slice.32, bf16[1,88,2048]{2,1,0:T(8,128)(2,1)S(1)} %get-tuple-element.295, bf16[2,88,16384]{2,1,0:T(8,128)(2,1)} %get-tuple-element.294, s32[]{:T(128)S(6)} %select_n.132), kind=kOutput, calls=%fused_computation.5.clone.1 | convolution fusion | flops 377485312 | bytes 8949764 | tf_op jit(solution)/shard_map/while/body/eval_jaxpr/hdq,hdk->hqk/dot_general | solution.py:65
  206.0 5.9 %fusion.49 = f32[1,88,2048]{2,1,0:T(8,128)S(1)} fusion(f32[1024,2048]{1,0:T(8,128)} %get-tuple-element.259, f32[2048]{0:T(1024)S(1)} %bitcast.110, s32[2048]{0:T(1024)S(1)} %get-tuple-element.292, s32[1024]{0:T(1024)S(1)} %dynamic_slice.32, f32[1,88,2048]{2,1,0:T(8,128)S(1)} %get-tuple-element.278, f32[2048]{0:T(1024)S(1)} %bitcast.117, ...), kind=kOutput, calls=%fused_computation.12.clone.1 | convolution fusion | flops 380125184 | bytes 10039305 | tf_op jit(solution)/shard_map/while/body/eval_jaxpr/hqk,hdk->hdq/dot_general | solution.py:73
  212.0 5.6 %fusion.45 = (f32[2048]{0:T(1024)S(1)}, f32[1024,2048]{1,0:T(8,128)}) fusion(s32[2048]{0:T(1024)S(1)} %get-tuple-element.292, s32[1024]{0:T(1024)S(1)} %dynamic_slice.32, bf16[1,88,2048]{2,1,0:T(8,128)(2,1)S(1)} %get-tuple-element.295, bf16[2,88,16384]{2,1,0:T(8,128)(2,1)} %get-tuple-element.294, s32[]{:T(128)S(6)} %select_n.132), kind=kOutput, calls=%fused_computation.5.clone.1 | convolution fusion | flops 377485312 | bytes 8949764 | tf_op jit(solution)/shard_map/while/body/eval_jaxpr/hdq,hdk->hqk/dot_general | solution.py:65
  227.8 5.6 %fusion.45 = (f32[2048]{0:T(1024)S(1)}, f32[1024,2048]{1,0:T(8,128)}) fusion(s32[2048]{0:T(1024)S(1)} %get-tuple-element.292, s32[1024]{0:T(1024)S(1)} %dynamic_slice.32, bf16[1,88,2048]{2,1,0:T(8,128)(2,1)S(1)} %get-tuple-element.295, bf16[2,88,16384]{2,1,0:T(8,128)(2,1)} %get-tuple-element.294, s32[]{:T(128)S(6)} %select_n.132), kind=kOutput, calls=%fused_computation.5.clone.1 | convolution fusion | flops 377485312 | bytes 8949764 | tf_op jit(solution)/shard_map/while/body/eval_jaxpr/hdq,hdk->hqk/dot_general | solution.py:65
  233.4 5.9 %fusion.47 = f32[2048]{0:T(1024)S(1)} fusion(f32[1024,2048]{1,0:T(8,128)} %get-tuple-element.259, f32[2048]{0:T(1024)S(1)} %bitcast.109, s32[2048]{0:T(1024)S(1)} %get-tuple-element.292, s32[1024]{0:T(1024)S(1)} %dynamic_slice.32), kind=kLoop, calls=%fused_computation.9.clone.1 | loop fusion | flops 10483712 | bytes 8417280 | tf_op jit(solution)/shard_map/while/body/eval_jaxpr/reduce_sum | solution.py:72
  244.8 5.6 %fusion.45 = (f32[2048]{0:T(1024)S(1)}, f32[1024,2048]{1,0:T(8,128)}) fusion(s32[2048]{0:T(1024)S(1)} %get-tuple-element.292, s32[1024]{0:T(1024)S(1)} %dynamic_slice.32, bf16[1,88,2048]{2,1,0:T(8,128)(2,1)S(1)} %get-tuple-element.295, bf16[2,88,16384]{2,1,0:T(8,128)(2,1)} %get-tuple-element.294, s32[]{:T(128)S(6)} %select_n.132), kind=kOutput, calls=%fused_computation.5.clone.1 | convolution fusion | flops 377485312 | bytes 8949764 | tf_op jit(solution)/shard_map/while/body/eval_jaxpr/hdq,hdk->hqk/dot_general | solution.py:65
  255.2 5.7 %fusion.49 = f32[1,88,2048]{2,1,0:T(8,128)S(1)} fusion(f32[1024,2048]{1,0:T(8,128)} %get-tuple-element.259, f32[2048]{0:T(1024)S(1)} %bitcast.110, s32[2048]{0:T(1024)S(1)} %get-tuple-element.292, s32[1024]{0:T(1024)S(1)} %dynamic_slice.32, f32[1,88,2048]{2,1,0:T(8,128)S(1)} %get-tuple-element.278, f32[2048]{0:T(1024)S(1)} %bitcast.117, ...), kind=kOutput, calls=%fused_computation.12.clone.1 | convolution fusion | flops 380125184 | bytes 10039305 | tf_op jit(solution)/shard_map/while/body/eval_jaxpr/hqk,hdk->hdq/dot_general | solution.py:73
  261.0 5.6 %fusion.45 = (f32[2048]{0:T(1024)S(1)}, f32[1024,2048]{1,0:T(8,128)}) fusion(s32[2048]{0:T(1024)S(1)} %get-tuple-element.292, s32[1024]{0:T(1024)S(1)} %dynamic_slice.32, bf16[1,88,2048]{2,1,0:T(8,128)(2,1)S(1)} %get-tuple-element.295, bf16[2,88,16384]{2,1,0:T(8,128)(2,1)} %get-tuple-element.294, s32[]{:T(128)S(6)} %select_n.132), kind=kOutput, calls=%fused_computation.5.clone.1 | convolution fusion | flops 377485312 | bytes 8949764 | tf_op jit(solution)/shard_map/while/body/eval_jaxpr/hdq,hdk->hqk/dot_general | solution.py:65
  271.4 5.7 %fusion.49 = f32[1,88,2048]{2,1,0:T(8,128)S(1)} fusion(f32[1024,2048]{1,0:T(8,128)} %get-tuple-element.259, f32[2048]{0:T(1024)S(1)} %bitcast.110, s32[2048]{0:T(1024)S(1)} %get-tuple-element.292, s32[1024]{0:T(1024)S(1)} %dynamic_slice.32, f32[1,88,2048]{2,1,0:T(8,128)S(1)} %get-tuple-element.278, f32[2048]{0:T(1024)S(1)} %bitcast.117, ...), kind=kOutput, calls=%fused_computation.12.clone.1 | convolution fusion | flops 380125184 | bytes 10039305 | tf_op jit(solution)/shard_map/while/body/eval_jaxpr/hqk,hdk->hdq/dot_general | solution.py:73
  277.1 5.6 %fusion.45 = (f32[2048]{0:T(1024)S(1)}, f32[1024,2048]{1,0:T(8,128)}) fusion(s32[2048]{0:T(1024)S(1)} %get-tuple-element.292, s32[1024]{0:T(1024)S(1)} %dynamic_slice.32, bf16[1,88,2048]{2,1,0:T(8,128)(2,1)S(1)} %get-tuple-element.295, bf16[2,88,16384]{2,1,0:T(8,128)(2,1)} %get-tuple-element.294, s32[]{:T(128)S(6)} %select_n.132), kind=kOutput, calls=%fused_computation.5.clone.1 | convolution fusion | flops 377485312 | bytes 8949764 | tf_op jit(solution)/shard_map/while/body/eval_jaxpr/hdq,hdk->hqk/dot_general | solution.py:65
  292.9 5.6 %fusion.45 = (f32[2048]{0:T(1024)S(1)}, f32[1024,2048]{1,0:T(8,128)}) fusion(s32[2048]{0:T(1024)S(1)} %get-tuple-element.292, s32[1024]{0:T(1024)S(1)} %dynamic_slice.32, bf16[1,88,2048]{2,1,0:T(8,128)(2,1)S(1)} %get-tuple-element.295, bf16[2,88,16384]{2,1,0:T(8,128)(2,1)} %get-tuple-element.294, s32[]{:T(128)S(6)} %select_n.132), kind=kOutput, calls=%fused_computation.5.clone.1 | convolution fusion | flops 377485312 | bytes 8949764 | tf_op jit(solution)/shard_map/while/body/eval_jaxpr/hdq,hdk->hqk/dot_general | solution.py:65
  324.2 5.6 %fusion.45 = (f32[2048]{0:T(1024)S(1)}, f32[1024,2048]{1,0:T(8,128)}) fusion(s32[2048]{0:T(1024)S(1)} %get-tuple-element.292, s32[1024]{0:T(1024)S(1)} %dynamic_slice.32, bf16[1,88,2048]{2,1,0:T(8,128)(2,1)S(1)} %get-tuple-element.295, bf16[2,88,16384]{2,1,0:T(8,128)(2,1)} %get-tuple-element.294, s32[]{:T(128)S(6)} %select_n.132), kind=kOutput, calls=%fused_computation.5.clone.1 | convolution fusion | flops 377485312 | bytes 8949764 | tf_op jit(solution)/shard_map/while/body/eval_jaxpr/hdq,hdk->hqk/dot_general | solution.py:65
  403.5 6.1 %all-to-all-start = ((bf16[88,16,128]{2,0,1:T(8,128)(2,1)}), bf16[88,16,128]{2,0,1:T(8,128)(2,1)S(1)}, u32[]{:S(2)}, u32[]{:S(2)}) async-start(bf16[88,16,128]{2,0,1:T(8,128)(2,1)} %copy.32), calls=%async_computation | async-start | bytes 720896 | tf_op jit(solution)/shard_map/all_to_all | solution.py:102
  409.7 7.7 %convert_element_type.50 = f32[1408,2048]{0,1:T(8,128)} convert(bf16[1408,2048]{0,1:T(8,128)(2,1)} %copy.28) | non-fusion elementwise | flops 2883584 | bytes 17301504 | tf_op jit(solution)/shard_map/convert_element_type | solution.py:33
  423.1 8.8 %fusion.23 = bf16[32,1408]{1,0:T(8,128)(2,1)} fusion(bf16[4,1408,1408]{2,1,0:T(8,128)(2,1)} %all-gather.12.cloned.1.call-done, bf16[1408,32,4]{0,2,1:T(4,128)(2,1)S(1)} %reshape.212), kind=kOutput, calls=%fused_computation.36 | convolution fusion | flops 507555840 | bytes 16310272 | tf_op jit(solution)/shard_map/fgi,ifd->gd/dot_general | solution.py:118
  433.3 41.2 %all-gather.14.cloned.1.call-done = bf16[512,1408]{1,0:T(8,128)(2,1)} async-done(((bf16[32,1408]{1,0:T(8,128)(2,1)}), bf16[512,1408]{1,0:T(8,128)(2,1)}) %all-gather.14.cloned.1.call-update) | async-done | bytes 1441808 | tf_op jit(solution)/shard_map/all_gather | solution.py:119
  (156 shorter events, 214.1 us)
Async XLA Ops:
  6.5 86.1 %copy-start = (bf16[2,88,1408]{2,1,0:T(8,128)(2,1)S(1)}, bf16[2,88,1408]{2,1,0:T(8,128)(2,1)}, u32[]{:S(2)}) copy-start(bf16[2,88,1408]{2,1,0:T(8,128)(2,1)} %param.16) | copy-start | bytes 1486852
  6.5 64.2 %all-gather.6.cloned.1.call-start = ((), (), s32[]{:S(2)}) async-start(), calls=%async_computation.1 | async-start | bytes 6127616 | tf_op jit(solution)/shard_map/all_gather | solution.py:31
  7.3 134.4 %all-gather.8.cloned.1.call-start = ((), (), s32[]{:S(2)}) async-start(), calls=%async_computation.2 | async-start | bytes 6782976 | tf_op jit(solution)/shard_map/all_gather | solution.py:56
  79.1 4.5 copy-start.2
  87.6 15.2 %copy-start.4 = (bf16[88,1408]{1,0:T(8,128)(2,1)S(1)}, bf16[88,1408]{1,0:T(8,128)(2,1)}, u32[]{:S(2)}) copy-start(bf16[88,1408]{1,0:T(8,128)(2,1)} %param.15) | copy-start | bytes 743428
  101.8 315.6 %all-gather.10.cloned.1.call-start = ((), (), s32[]{:S(2)}) async-start(), calls=%async_computation.3 | async-start | bytes 4212736 | tf_op jit(solution)/shard_map/all_gather | solution.py:32
  102.5 320.5 %all-gather.12.cloned.1.call-start = ((), (), s32[]{:S(2)}) async-start(), calls=%async_computation.4 | async-start | bytes 16850944 | tf_op jit(solution)/shard_map/all_gather | solution.py:116
  102.8 45.7 %copy-start.3 = (s32[2048]{0:T(1024)S(1)}, s32[2048]{0:T(1024)}, u32[]{:S(2)}) copy-start(s32[2048]{0:T(1024)} %param.19) | copy-start | bytes 24580
  148.5 261.2 %copy-start.5 = (bf16[1408]{0:T(1024)(128)(2,1)S(1)}, bf16[1408]{0:T(1024)(128)(2,1)}, u32[]{:S(2)}) copy-start(bf16[1408]{0:T(1024)(128)(2,1)} %param.21) | copy-start | bytes 8452
  403.5 16.0 %all-to-all-start = ((bf16[88,16,128]{2,0,1:T(8,128)(2,1)}), bf16[88,16,128]{2,0,1:T(8,128)(2,1)S(1)}, u32[]{:S(2)}, u32[]{:S(2)}) async-start(bf16[88,16,128]{2,0,1:T(8,128)(2,1)} %copy.32), calls=%async_computation | async-start | bytes 720896 | tf_op jit(solution)/shard_map/all_to_all | solution.py:102
  409.6 64.9 %all-gather.14.cloned.1.call-start = ((), (), s32[]{:S(2)}) async-start(), calls=%async_computation.5 | async-start | bytes 1531904 | tf_op jit(solution)/shard_map/all_gather | solution.py:119
  422.9 54.9 %copy-start.1 = (bf16[2,88,1408]{2,1,0:T(8,128)(2,1)S(1)}, bf16[2,88,1408]{2,1,0:T(8,128)(2,1)}, u32[]{:S(2)}) copy-start(bf16[2,88,1408]{2,1,0:T(8,128)(2,1)} %param.16) | copy-start | bytes 1486852
Sparse Core Ops, SparseCore 0:
  9.5 61.1 all-gather.5
  101.9 39.7 all-gather.7
  143.8 50.4 all-gather.9
  196.4 106.0 all-gather.11
  432.0 42.4 all-gather.13
where the time goes:
time: 486 us; the launch traced here: 484 us
  matrix products  194 us (40%)
  waiting for transfers between devices  137 us (28%)
  other arithmetic  99.7 us (21%)
  local copies, waits for them, and re-layouts  33 us (7%)
  between operations  13.4 us (3%)
  starting transfers between devices  6.4 us (1%)
    dot_general x16, matrix products, take_block(): jnp.einsum('hdq,hdk->hqk', query_heads, key_block, preferred_element_type...  89.1 us
    dot_general x16, matrix products, take_block(): jnp.einsum('hqk,hdk->hdq', weights_exp.astype(jnp.bfloat16), value_block,...  87.5 us
    reduce_sum x16, other arithmetic, take_block(): running_sum = running_sum * factor + jnp.sum(weights_exp, axis=2)  75.4 us
    all_gather x1, waiting for transfers between devices, on_device(): full_rows = lax.all_gather(hidden, 'col', axis=0, tiled=True)  58.2 us
    all_gather x1, waiting for transfers between devices, on_device(): lax.all_gather(merged_here.astype(jnp.bfloat16), 'col', axis=0, tiled=True)  41.2 us
    all_gather x1, waiting for transfers between devices, on_device(): pair_all = lax.all_gather(pair_local, 'row', axis=1, tiled=True)  34.2 us
  transfers between devices with their start and end apart: 6, of which 4 were waited for; matrix products, arithmetic and copies ran while one was open for 58% of the time, Pallas kernels for 0%

commit v1 on v0

--- a/solution.py
+++ b/solution.py
@@ -7,6 +7,11 @@
 EPSILON = 1e-06
 MASKED = -1e30
 KEY_BLOCK = 1024
+
+
+def gather_over(x, mesh_axis, dim):
+    outgoing = jnp.stack([x] * lax.axis_size(mesh_axis))
+    return jnp.concatenate(lax.all_to_all(outgoing, mesh_axis, 0, 0), axis=dim)
 
 
 def on_device(
@@ -116,7 +121,7 @@
     merge_full = lax.all_gather(merge_weight, "col", axis=1, tiled=True)
     grouped = merger_chunk.reshape(model_width, chunk // 4, 4)
     merged_here = jnp.einsum("fgi,ifd->gd", grouped, merge_full, preferred_element_type=jnp.float32)
-    merged_all = lax.all_gather(merged_here.astype(jnp.bfloat16), "col", axis=0, tiled=True)
+    merged_all = gather_over(merged_here.astype(jnp.bfloat16), "col", 0)
     wanted_rows = lax.dynamic_index_in_dim(requests[0], col_index, 0, keepdims=False)
     is_valid = wanted_rows >= 0
     safe_index = jnp.where(is_valid, wanted_rows, 0)

time: 486 us -> 469 us (0.965)
  waiting for transfers between devices: 137 us -> 117 us
  starting transfers between devices: 6.4 us -> 11.3 us
    all_gather x1 -> x0, waiting for transfers between devices: 41.2 us -> none  [on_device(): lax.all_gather(merged_here.astype(jnp.bfloat16), 'col', axis=0, tiled=True)]
    all_to_all x0 -> x1, waiting for transfers between devices: none -> 20.5 us  [gather_over(): return jnp.concatenate(lax.all_to_all(outgoing, mesh_axis, 0, 0), axis=dim)]
    all_to_all x0 -> x1, starting transfers between devices: none -> 4.97 us  [gather_over(): return jnp.concatenate(lax.all_to_all(outgoing, mesh_axis, 0, 0), axis=dim)]
  transfers between devices with their start and end apart: 6 -> 6, of which waited for: 4 -> 4; matrix products, arithmetic and copies ran while one was open for 58% -> 61% of each run, Pallas kernels for 0% -> 0%
where the time goes in v1:
time: 469 us; the launch traced here: 468 us
  matrix products  193 us (41%)
  waiting for transfers between devices  117 us (25%)
  other arithmetic  99.7 us (21%)
  local copies, waits for them, and re-layouts  32.5 us (7%)
  between operations  13.4 us (3%)
  starting transfers between devices  11.3 us (2%)
    dot_general x16, matrix products, take_block(): jnp.einsum('hdq,hdk->hqk', query_heads, key_block, preferred_element_type...  89.2 us
    dot_general x16, matrix products, take_block(): jnp.einsum('hqk,hdk->hdq', weights_exp.astype(jnp.bfloat16), value_block,...  87.5 us
    reduce_sum x16, other arithmetic, take_block(): running_sum = running_sum * factor + jnp.sum(weights_exp, axis=2)  75.4 us
    all_gather x1, waiting for transfers between devices, on_device(): full_rows = lax.all_gather(hidden, 'col', axis=0, tiled=True)  58.2 us
    all_gather x1, waiting for transfers between devices, on_device(): pair_all = lax.all_gather(pair_local, 'row', axis=1, tiled=True)  34.2 us
    all_to_all x1, waiting for transfers between devices, gather_over(): return jnp.concatenate(lax.all_to_all(outgoing, mesh_axis, 0, 0), axis=dim)  20.5 us
  transfers between devices with their start and end apart: 6, of which 4 were waited for; matrix products, arithmetic and copies ran while one was open for 61% of the time, Pallas kernels for 0%

profile of v1, /device:TPU:0, one launch (start us, length us, event | category | flops | bytes accessed | tf_op | source)
XLA Modules:
  0.0 467.5 jit_solution(7236269267447843662)
XLA Ops:
  12.5 58.2 %all-gather.5.cloned.1.call-done = bf16[1408,2048]{1,0:T(8,128)(2,1)} async-done(((bf16[88,2048]{1,0:T(8,128)(2,1)}), bf16[1408,2048]{1,0:T(8,128)(2,1)}) %all-gather.5.cloned.1.call-update) | async-done | bytes 5767184 | tf_op jit(solution)/shard_map/all_gather | solution.py:36
  70.7 8.3 %copy.28 = bf16[1408,2048]{0,1:T(8,128)(2,1)} copy(bf16[1408,2048]{1,0:T(8,128)(2,1)} %all-gather.5.cloned.1.call-done) | data formatting | bytes 11534336 | tf_op jit(solution)/shard_map/all_gather | solution.py:36
  93.2 6.9 %scatter_fusion = bf16[2,88,2048]{1,0,2:T(2,128)(2,1)S(1)} fusion(bf16[2,88,2048]{1,0,2:T(2,128)(2,1)S(1)} %copy.30, s32[200]{0:T(256)S(1)} %bitcast.124, bf16[200,2,88]{2,1,0:T(2,128)(2,1)S(1)} %bitcast.117), kind=kCustom, calls=%fused_computation.2 | custom fusion | bytes 212000 | tf_op jit(solution)/shard_map/scatter | solution.py:55
  107.5 34.2 %all-gather.7.cloned.1.call-done = bf16[177,16384]{1,0:T(8,128)(2,1)} async-done(((bf16[177,2048]{1,0:T(8,128)(2,1)}), bf16[177,16384]{1,0:T(8,128)(2,1)}) %all-gather.7.cloned.1.call-update) | async-done | bytes 5799952 | tf_op jit(solution)/shard_map/all_gather | solution.py:61
  141.7 5.8 %slice.29 = bf16[176,16384]{1,0:T(8,128)(2,1)} slice(bf16[177,16384]{1,0:T(8,128)(2,1)} %all-gather.7.cloned.1.call-done), slice={[0:176], [0:16384]} | slice | bytes 11534336 | tf_op jit(solution)/shard_map/slice | solution.py:62
  148.5 254.0 %while.18 = (s32[]{:T(128)}, f32[1,2048]{1,0:T(1,128)S(1)}, f32[1,2048]{1,0:T(1,128)S(1)}, f32[1,88,2048]{2,1,0:T(8,128)S(1)}, s32[2048]{0:T(1024)S(1)}, /*index...) while((s32[]{:T(128)}, f32[1,2048]{1,0:T(1,128)S(1)}, ...), condition=%wide.region_6.7_spmd.clone, body=%wide.region_3.0_spmd.clone.sunk | while | flops 768108544 | bytes 27504848 | solution.py:102
  148.6 5.6 %fusion.45 = (f32[2048]{0:T(1024)S(1)}, f32[1024,2048]{1,0:T(8,128)}) fusion(s32[2048]{0:T(1024)S(1)} %get-tuple-element.292, s32[1024]{0:T(1024)S(1)} %dynamic_slice.32, bf16[1,88,2048]{2,1,0:T(8,128)(2,1)S(1)} %get-tuple-element.295, bf16[2,88,16384]{2,1,0:T(8,128)(2,1)} %get-tuple-element.294, s32[]{:T(128)S(6)} %select_n.132), kind=kOutput, calls=%fused_computation.5.clone.1 | convolution fusion | flops 377485312 | bytes 8949764 | tf_op jit(solution)/shard_map/while/body/eval_jaxpr/hdq,hdk->hqk/dot_general | solution.py:70
  164.3 5.6 %fusion.45 = (f32[2048]{0:T(1024)S(1)}, f32[1024,2048]{1,0:T(8,128)}) fusion(s32[2048]{0:T(1024)S(1)} %get-tuple-element.292, s32[1024]{0:T(1024)S(1)} %dynamic_slice.32, bf16[1,88,2048]{2,1,0:T(8,128)(2,1)S(1)} %get-tuple-element.295, bf16[2,88,16384]{2,1,0:T(8,128)(2,1)} %get-tuple-element.294, s32[]{:T(128)S(6)} %select_n.132), kind=kOutput, calls=%fused_computation.5.clone.1 | convolution fusion | flops 377485312 | bytes 8949764 | tf_op jit(solution)/shard_map/while/body/eval_jaxpr/hdq,hdk->hqk/dot_general | solution.py:70
  180.0 5.6 %fusion.45 = (f32[2048]{0:T(1024)S(1)}, f32[1024,2048]{1,0:T(8,128)}) fusion(s32[2048]{0:T(1024)S(1)} %get-tuple-element.292, s32[1024]{0:T(1024)S(1)} %dynamic_slice.32, bf16[1,88,2048]{2,1,0:T(8,128)(2,1)S(1)} %get-tuple-element.295, bf16[2,88,16384]{2,1,0:T(8,128)(2,1)} %get-tuple-element.294, s32[]{:T(128)S(6)} %select_n.132), kind=kOutput, calls=%fused_computation.5.clone.1 | convolution fusion | flops 377485312 | bytes 8949764 | tf_op jit(solution)/shard_map/while/body/eval_jaxpr/hdq,hdk->hqk/dot_general | solution.py:70
  195.8 5.6 %fusion.45 = (f32[2048]{0:T(1024)S(1)}, f32[1024,2048]{1,0:T(8,128)}) fusion(s32[2048]{0:T(1024)S(1)} %get-tuple-element.292, s32[1024]{0:T(1024)S(1)} %dynamic_slice.32, bf16[1,88,2048]{2,1,0:T(8,128)(2,1)S(1)} %get-tuple-element.295, bf16[2,88,16384]{2,1,0:T(8,128)(2,1)} %get-tuple-element.294, s32[]{:T(128)S(6)} %select_n.132), kind=kOutput, calls=%fused_computation.5.clone.1 | convolution fusion | flops 377485312 | bytes 8949764 | tf_op jit(solution)/shard_map/while/body/eval_jaxpr/hdq,hdk->hqk/dot_general | solution.py:70
  206.1 5.9 %fusion.49 = f32[1,88,2048]{2,1,0:T(8,128)S(1)} fusion(f32[1024,2048]{1,0:T(8,128)} %get-tuple-element.259, f32[2048]{0:T(1024)S(1)} %bitcast.112, s32[2048]{0:T(1024)S(1)} %get-tuple-element.292, s32[1024]{0:T(1024)S(1)} %dynamic_slice.32, f32[1,88,2048]{2,1,0:T(8,128)S(1)} %get-tuple-element.278, f32[2048]{0:T(1024)S(1)} %bitcast.119, ...), kind=kOutput, calls=%fused_computation.12.clone.1 | convolution fusion | flops 380125184 | bytes 10039305 | tf_op jit(solution)/shard_map/while/body/eval_jaxpr/hqk,hdk->hdq/dot_general | solution.py:78
  212.0 5.6 %fusion.45 = (f32[2048]{0:T(1024)S(1)}, f32[1024,2048]{1,0:T(8,128)}) fusion(s32[2048]{0:T(1024)S(1)} %get-tuple-element.292, s32[1024]{0:T(1024)S(1)} %dynamic_slice.32, bf16[1,88,2048]{2,1,0:T(8,128)(2,1)S(1)} %get-tuple-element.295, bf16[2,88,16384]{2,1,0:T(8,128)(2,1)} %get-tuple-element.294, s32[]{:T(128)S(6)} %select_n.132), kind=kOutput, calls=%fused_computation.5.clone.1 | convolution fusion | flops 377485312 | bytes 8949764 | tf_op jit(solution)/shard_map/while/body/eval_jaxpr/hdq,hdk->hqk/dot_general | solution.py:70
  227.8 5.6 %fusion.45 = (f32[2048]{0:T(1024)S(1)}, f32[1024,2048]{1,0:T(8,128)}) fusion(s32[2048]{0:T(1024)S(1)} %get-tuple-element.292, s32[1024]{0:T(1024)S(1)} %dynamic_slice.32, bf16[1,88,2048]{2,1,0:T(8,128)(2,1)S(1)} %get-tuple-element.295, bf16[2,88,16384]{2,1,0:T(8,128)(2,1)} %get-tuple-element.294, s32[]{:T(128)S(6)} %select_n.132), kind=kOutput, calls=%fused_computation.5.clone.1 | convolution fusion | flops 377485312 | bytes 8949764 | tf_op jit(solution)/shard_map/while/body/eval_jaxpr/hdq,hdk->hqk/dot_general | solution.py:70
  233.4 5.9 %fusion.47 = f32[2048]{0:T(1024)S(1)} fusion(f32[1024,2048]{1,0:T(8,128)} %get-tuple-element.259, f32[2048]{0:T(1024)S(1)} %bitcast.111, s32[2048]{0:T(1024)S(1)} %get-tuple-element.292, s32[1024]{0:T(1024)S(1)} %dynamic_slice.32), kind=kLoop, calls=%fused_computation.9.clone.1 | loop fusion | flops 10483712 | bytes 8417280 | tf_op jit(solution)/shard_map/while/body/eval_jaxpr/reduce_sum | solution.py:77
  244.8 5.6 %fusion.45 = (f32[2048]{0:T(1024)S(1)}, f32[1024,2048]{1,0:T(8,128)}) fusion(s32[2048]{0:T(1024)S(1)} %get-tuple-element.292, s32[1024]{0:T(1024)S(1)} %dynamic_slice.32, bf16[1,88,2048]{2,1,0:T(8,128)(2,1)S(1)} %get-tuple-element.295, bf16[2,88,16384]{2,1,0:T(8,128)(2,1)} %get-tuple-element.294, s32[]{:T(128)S(6)} %select_n.132), kind=kOutput, calls=%fused_computation.5.clone.1 | convolution fusion | flops 377485312 | bytes 8949764 | tf_op jit(solution)/shard_map/while/body/eval_jaxpr/hdq,hdk->hqk/dot_general | solution.py:70
  255.3 5.7 %fusion.49 = f32[1,88,2048]{2,1,0:T(8,128)S(1)} fusion(f32[1024,2048]{1,0:T(8,128)} %get-tuple-element.259, f32[2048]{0:T(1024)S(1)} %bitcast.112, s32[2048]{0:T(1024)S(1)} %get-tuple-element.292, s32[1024]{0:T(1024)S(1)} %dynamic_slice.32, f32[1,88,2048]{2,1,0:T(8,128)S(1)} %get-tuple-element.278, f32[2048]{0:T(1024)S(1)} %bitcast.119, ...), kind=kOutput, calls=%fused_computation.12.clone.1 | convolution fusion | flops 380125184 | bytes 10039305 | tf_op jit(solution)/shard_map/while/body/eval_jaxpr/hqk,hdk->hdq/dot_general | solution.py:78
  261.0 5.6 %fusion.45 = (f32[2048]{0:T(1024)S(1)}, f32[1024,2048]{1,0:T(8,128)}) fusion(s32[2048]{0:T(1024)S(1)} %get-tuple-element.292, s32[1024]{0:T(1024)S(1)} %dynamic_slice.32, bf16[1,88,2048]{2,1,0:T(8,128)(2,1)S(1)} %get-tuple-element.295, bf16[2,88,16384]{2,1,0:T(8,128)(2,1)} %get-tuple-element.294, s32[]{:T(128)S(6)} %select_n.132), kind=kOutput, calls=%fused_computation.5.clone.1 | convolution fusion | flops 377485312 | bytes 8949764 | tf_op jit(solution)/shard_map/while/body/eval_jaxpr/hdq,hdk->hqk/dot_general | solution.py:70
  271.4 5.7 %fusion.49 = f32[1,88,2048]{2,1,0:T(8,128)S(1)} fusion(f32[1024,2048]{1,0:T(8,128)} %get-tuple-element.259, f32[2048]{0:T(1024)S(1)} %bitcast.112, s32[2048]{0:T(1024)S(1)} %get-tuple-element.292, s32[1024]{0:T(1024)S(1)} %dynamic_slice.32, f32[1,88,2048]{2,1,0:T(8,128)S(1)} %get-tuple-element.278, f32[2048]{0:T(1024)S(1)} %bitcast.119, ...), kind=kOutput, calls=%fused_computation.12.clone.1 | convolution fusion | flops 380125184 | bytes 10039305 | tf_op jit(solution)/shard_map/while/body/eval_jaxpr/hqk,hdk->hdq/dot_general | solution.py:78
  277.1 5.6 %fusion.45 = (f32[2048]{0:T(1024)S(1)}, f32[1024,2048]{1,0:T(8,128)}) fusion(s32[2048]{0:T(1024)S(1)} %get-tuple-element.292, s32[1024]{0:T(1024)S(1)} %dynamic_slice.32, bf16[1,88,2048]{2,1,0:T(8,128)(2,1)S(1)} %get-tuple-element.295, bf16[2,88,16384]{2,1,0:T(8,128)(2,1)} %get-tuple-element.294, s32[]{:T(128)S(6)} %select_n.132), kind=kOutput, calls=%fused_computation.5.clone.1 | convolution fusion | flops 377485312 | bytes 8949764 | tf_op jit(solution)/shard_map/while/body/eval_jaxpr/hdq,hdk->hqk/dot_general | solution.py:70
  308.6 5.6 %fusion.45 = (f32[2048]{0:T(1024)S(1)}, f32[1024,2048]{1,0:T(8,128)}) fusion(s32[2048]{0:T(1024)S(1)} %get-tuple-element.292, s32[1024]{0:T(1024)S(1)} %dynamic_slice.32, bf16[1,88,2048]{2,1,0:T(8,128)(2,1)S(1)} %get-tuple-element.295, bf16[2,88,16384]{2,1,0:T(8,128)(2,1)} %get-tuple-element.294, s32[]{:T(128)S(6)} %select_n.132), kind=kOutput, calls=%fused_computation.5.clone.1 | convolution fusion | flops 377485312 | bytes 8949764 | tf_op jit(solution)/shard_map/while/body/eval_jaxpr/hdq,hdk->hqk/dot_general | solution.py:70
  403.6 6.1 %all-to-all-start = ((bf16[88,16,128]{2,0,1:T(8,128)(2,1)}), bf16[88,16,128]{2,0,1:T(8,128)(2,1)S(1)}, u32[]{:S(2)}, u32[]{:S(2)}) async-start(bf16[88,16,128]{2,0,1:T(8,128)(2,1)} %copy.32), calls=%async_computation | async-start | bytes 720896 | tf_op jit(solution)/shard_map/all_to_all | solution.py:107
  409.7 7.7 %convert_element_type.50 = f32[1408,2048]{0,1:T(8,128)} convert(bf16[1408,2048]{0,1:T(8,128)(2,1)} %copy.28) | non-fusion elementwise | flops 2883584 | bytes 17301504 | tf_op jit(solution)/shard_map/convert_element_type | solution.py:38
  423.1 8.1 %fusion.23 = bf16[32,1408]{1,0:T(8,128)(2,1)S(1)} fusion(bf16[4,1408,1408]{2,1,0:T(8,128)(2,1)} %all-gather.11.cloned.1.call-done, bf16[1408,32,4]{0,2,1:T(4,128)(2,1)S(1)} %reshape.217), kind=kOutput, calls=%fused_computation.36 | convolution fusion | flops 507555840 | bytes 16310272 | tf_op jit(solution)/shard_map/fgi,ifd->gd/dot_general | solution.py:123
  438.9 20.5 %all-to-all-done.1 = bf16[16,32,1408]{2,1,0:T(8,128)(2,1)S(1)} async-done(((bf16[16,32,1408]{2,1,0:T(8,128)(2,1)}), bf16[16,32,1408]{2,1,0:T(8,128)(2,1)S(1)}, u32[]{:S(2)}, u32[]{:S(2)}) %all-to-all-start.1) | async-done | bytes 1441824 | tf_op jit(solution)/shard_map/all_to_all | solution.py:14
  (156 shorter events, 218.5 us)
Async XLA Ops:
  6.5 86.1 %copy-start = (bf16[2,88,1408]{2,1,0:T(8,128)(2,1)S(1)}, bf16[2,88,1408]{2,1,0:T(8,128)(2,1)}, u32[]{:S(2)}) copy-start(bf16[2,88,1408]{2,1,0:T(8,128)(2,1)} %param.16) | copy-start | bytes 1486852
  6.5 64.2 %all-gather.5.cloned.1.call-start = ((), (), s32[]{:S(2)}) async-start(), calls=%async_computation.2 | async-start | bytes 6127616 | tf_op jit(solution)/shard_map/all_gather | solution.py:36
  7.3 134.5 %all-gather.7.cloned.1.call-start = ((), (), s32[]{:S(2)}) async-start(), calls=%async_computation.3 | async-start | bytes 6782976 | tf_op jit(solution)/shard_map/all_gather | solution.py:61
  79.1 4.5 copy-start.2
  87.6 15.2 %copy-start.4 = (bf16[88,1408]{1,0:T(8,128)(2,1)S(1)}, bf16[88,1408]{1,0:T(8,128)(2,1)}, u32[]{:S(2)}) copy-start(bf16[88,1408]{1,0:T(8,128)(2,1)} %param.15) | copy-start | bytes 743428
  101.8 315.5 %all-gather.9.cloned.1.call-start = ((), (), s32[]{:S(2)}) async-start(), calls=%async_computation.4 | async-start | bytes 4212736 | tf_op jit(solution)/shard_map/all_gather | solution.py:37
  102.6 320.6 %all-gather.11.cloned.1.call-start = ((), (), s32[]{:S(2)}) async-start(), calls=%async_computation.5 | async-start | bytes 16850944 | tf_op jit(solution)/shard_map/all_gather | solution.py:121
  102.8 45.7 %copy-start.3 = (s32[2048]{0:T(1024)S(1)}, s32[2048]{0:T(1024)}, u32[]{:S(2)}) copy-start(s32[2048]{0:T(1024)} %param.19) | copy-start | bytes 24580
  148.5 261.1 %copy-start.5 = (bf16[1408]{0:T(1024)(128)(2,1)S(1)}, bf16[1408]{0:T(1024)(128)(2,1)}, u32[]{:S(2)}) copy-start(bf16[1408]{0:T(1024)(128)(2,1)} %param.21) | copy-start | bytes 8452
  403.6 16.0 %all-to-all-start = ((bf16[88,16,128]{2,0,1:T(8,128)(2,1)}), bf16[88,16,128]{2,0,1:T(8,128)(2,1)S(1)}, u32[]{:S(2)}, u32[]{:S(2)}) async-start(bf16[88,16,128]{2,0,1:T(8,128)(2,1)} %copy.32), calls=%async_computation | async-start | bytes 720896 | tf_op jit(solution)/shard_map/all_to_all | solution.py:107
  423.0 38.0 %copy-start.1 = (bf16[2,88,1408]{2,1,0:T(8,128)(2,1)S(1)}, bf16[2,88,1408]{2,1,0:T(8,128)(2,1)}, u32[]{:S(2)}) copy-start(bf16[2,88,1408]{2,1,0:T(8,128)(2,1)} %param.16) | copy-start | bytes 1486852
  432.5 26.9 %all-to-all-start.1 = ((bf16[16,32,1408]{2,1,0:T(8,128)(2,1)}), bf16[16,32,1408]{2,1,0:T(8,128)(2,1)S(1)}, u32[]{:S(2)}, u32[]{:S(2)}) async-start(bf16[16,32,1408]{2,1,0:T(8,128)(2,1)} %stack.2), calls=%async_computation.1 | async-start | bytes 2883584 | tf_op jit(solution)/shard_map/all_to_all | solution.py:14
Sparse Core Ops, SparseCore 0:
  9.5 61.1 all-gather.4
  101.9 39.7 all-gather.6
  143.9 50.4 all-gather.8
  196.4 106.0 all-gather.10
